TPU v7x, 256 devices: a whole 4x4x8 slice. The times are simulated.
256 devices in a mesh: tp: 2 (over z_lo), sp: 32 (over x, y, core), dp: 4 (over z_hi).
Axes of the slice: x: 4, y: 4, z: 8 (z_hi: 4, z_lo: 2; z = z_hi * 2 + z_lo), core: 2. Of those that a mesh axis runs over, the one named last changes fastest.
Arguments:
- queries: bfloat16 [16384, 4096], P(('dp', 'sp'), 'tp'), parts along dimension 0, may hold values from -256 to 256
- key_projection_rows: bfloat16 [16384, 512], P(('dp', 'sp'), 'tp'), parts along dimension 0, may hold values from -8 to 8
- values: bfloat16 [16384, 512], P(('dp', 'sp'), 'tp'), parts along dimension 0, may hold values from -6 to 6
- segment_ids: int32 [16384], P('dp'), parts along dimension 0, may hold values from 0 to 11, never falling along the last dimension, each value on 1 to 1024 neighbouring positions
- residual: bfloat16 [16384, 8192], P(('dp', 'tp'), 'sp'), parts along dimension 0, may hold values from -40 to 40
- out_weight: bfloat16 [4096, 8192], P('tp', 'sp'), may hold values from -0.09375 to 0.09375
- norm_gain: float32 [8192], P('sp'), may hold values from 0.1 to 1.9
- scale_exponent: int32 [8192], P('sp'), may hold values from 7 to 8
Outputs:
- hidden_out: bfloat16 [16384, 8192], P(('dp', 'tp'), 'sp'), parts along dimension 0
- quantized: bfloat16 [16384, 8192], P(('dp', 'tp'), 'sp'), parts along dimension 0
There are 4 independent parts, one for each index of `dp`. A program takes and returns all parts, laid end to end along the dimension named above; an argument that names none is the same for every part. Nothing has to cross between parts.
Inputs may be any that keep to these rules, and one draw needn't show every extreme that they name: `segment_ids`: never falls along the window; every document holds at most a quarter of the window's tokens, and one holds exactly that many.
All inputs are finite; a program needn't handle non-finite values.
Results may differ from a plain program's by a relative error of at most 0.0065.
Values may be sent and summed in bfloat16 or wider, within the bound.
No kernel may reach another device: no remote copies, remote signals or barrier semaphores. Data moves between devices by JAX's collectives and lax.ppermute only.
A program may use at most 64 MiB of HBM per device.

v0:
```python
import jax
import jax.numpy as jnp
from jax import lax
from jax.sharding import PartitionSpec as P

D = 8192
QUERY_HEAD_COUNT = 32
KEY_VALUE_HEADS = 4
HEAD_DIMENSION = 128
epsilon = 1e-05
limit_value = 448.0


def attend_item(query_block, key_block, value_block, query_pos, query_seg, segment_ids, key_pos):
    query_count = query_block.shape[0]
    block_rows = min(512, query_count)
    blocks = query_count // block_rows

    def one_block(packed):
        block_query, block_pos, block_seg = packed
        scores = lax.dot_general(
            block_query, key_block, (((1,), (1,)), ((), ())), preferred_element_type=jnp.float32
        ) * HEAD_DIMENSION ** (-0.5)
        visible = (key_pos[None, :] <= block_pos[:, None]) & (
            segment_ids[None, :] == block_seg[:, None]
        )
        scores = jnp.where(visible, scores, -1e30)
        largest = jnp.max(scores, axis=1, keepdims=True)
        weights = jnp.exp(scores - largest)
        row_total = jnp.sum(weights, axis=1, keepdims=True)
        probabilities = (weights / row_total).astype(jnp.bfloat16)
        return jnp.dot(probabilities, value_block, preferred_element_type=jnp.float32).astype(
            jnp.bfloat16
        )

    results = lax.map(
        one_block,
        (
            query_block.reshape(blocks, block_rows, HEAD_DIMENSION),
            query_pos.reshape(blocks, block_rows),
            query_seg.reshape(blocks, block_rows),
        ),
    )
    return results.reshape(query_count, HEAD_DIMENSION)


def body(
    queries,
    key_projection_rows,
    values,
    segment_ids,
    residual,
    out_weight,
    norm_gain,
    scale_exponent,
):
    sp_count = lax.axis_size("sp")
    token_rows = queries.shape[0]
    half_rows = token_rows // 2
    local_heads = queries.shape[1] // HEAD_DIMENSION
    item_count = 2 * local_heads
    per_device = item_count // sp_count
    window_token_rows = token_rows * sp_count
    query_count = window_token_rows // 2
    group_width = QUERY_HEAD_COUNT // KEY_VALUE_HEADS
    own_index = lax.axis_index("sp")
    query_items = jnp.transpose(
        queries.reshape(2, half_rows, local_heads, HEAD_DIMENSION), (0, 2, 1, 3)
    ).reshape(item_count, half_rows, HEAD_DIMENSION)
    query_recv = lax.all_to_all(query_items, "sp", split_axis=0, concat_axis=1, tiled=True)
    key_all, value_all = (
        lax.all_gather(key_projection_rows, "sp", axis=0, tiled=True),
        lax.all_gather(values, "sp", axis=0, tiled=True),
    )
    key_pos = jnp.arange(window_token_rows, dtype=jnp.int32)
    row_number = jnp.arange(query_count, dtype=jnp.int32)
    source_device = row_number // half_rows
    within = row_number % half_rows
    segment_grid = segment_ids.reshape(sp_count, 2, half_rows)
    number = 0
    item_index = own_index * per_device + number
    which_half = item_index // local_heads
    query_pos = source_device * token_rows + which_half * half_rows + within
    query_seg = lax.dynamic_index_in_dim(segment_grid, which_half, 1, keepdims=False).reshape(
        query_count
    )
    shared_rows = item_index % local_heads // group_width
    key_block = lax.dynamic_slice_in_dim(key_all, shared_rows * HEAD_DIMENSION, HEAD_DIMENSION, 1)
    value_block = lax.dynamic_slice_in_dim(
        value_all, shared_rows * HEAD_DIMENSION, HEAD_DIMENSION, 1
    )
    outputs = [
        attend_item(
            query_recv[number], key_block, value_block, query_pos, query_seg, segment_ids, key_pos
        )
    ]
    own_outputs = jnp.stack(outputs)
    column_count = out_weight.shape[1]
    start_sum = jnp.zeros((sp_count, 2, half_rows, column_count), jnp.float32)
    pieces = lax.all_gather(own_outputs, "sp", axis=0, tiled=True)

    def add_one(number, current):
        head_number = number % local_heads
        which_half = number // local_heads
        head_weight = lax.dynamic_slice_in_dim(
            out_weight, head_number * HEAD_DIMENSION, HEAD_DIMENSION, 0
        )
        chosen = lax.dynamic_index_in_dim(pieces, number, 0, keepdims=False)
        product_term = jnp.dot(chosen, head_weight, preferred_element_type=jnp.float32).reshape(
            sp_count, 1, half_rows, column_count
        )
        corner = (0, which_half, 0, 0)
        earlier = lax.dynamic_slice(current, corner, (sp_count, 1, half_rows, column_count))
        return lax.dynamic_update_slice(current, earlier + product_term, corner)

    combined = lax.fori_loop(0, pieces.shape[0], add_one, start_sum)
    flattened = combined.reshape(window_token_rows, column_count)
    share_rows = window_token_rows // lax.axis_size("tp")
    whole_sum = lax.psum(flattened, "tp")
    summed = lax.dynamic_slice_in_dim(whole_sum, lax.axis_index("tp") * share_rows, share_rows, 0)
    projected = summed.astype(jnp.bfloat16)
    hidden_out = (residual.astype(jnp.float32) + projected.astype(jnp.float32)).astype(jnp.bfloat16)
    widened = hidden_out.astype(jnp.float32)
    square_sum = lax.psum(jnp.sum(widened * widened, axis=1), "sp")
    mean_square = (square_sum / D)[:, None]
    normed = widened * lax.rsqrt(mean_square + epsilon) * norm_gain[None, :]
    clip_bound = (limit_value * jnp.exp2(-scale_exponent.astype(jnp.float32)))[None, :]
    quantized = jnp.clip(normed, -clip_bound, clip_bound).astype(jnp.bfloat16)
    return (hidden_out, quantized)


def solution(mesh):
    in_specs = (
        P(("dp", "sp"), "tp"),
        P(("dp", "sp"), "tp"),
        P(("dp", "sp"), "tp"),
        P("dp"),
        P(("dp", "tp"), "sp"),
        P("tp", "sp"),
        P("sp"),
        P("sp"),
    )
    out_specs = (P(("dp", "tp"), "sp"), P(("dp", "tp"), "sp"))
    return jax.shard_map(body, mesh=mesh, in_specs=in_specs, out_specs=out_specs, check_vma=False)
```

profile of v0, /device:TPU:1, one launch (start us, length us, event | category | flops | bytes accessed | tf_op | source)
XLA Modules:
  0.0 569.2 jit_solution(7606608849317972235)
XLA Ops:
  10.8 8.6 %all-to-all-start = ((bf16[32,64,128]{2,1,0:T(8,128)(2,1)}), bf16[32,64,128]{2,1,0:T(8,128)(2,1)S(1)}, u32[]{:S(2)}, u32[]{:S(2)}) async-start(bf16[32,64,128]{2,1,0:T(8,128)(2,1)} %bitcast.4), calls=%async_computation | async-start | bytes 1048576 | tf_op jit(solution)/shard_map/all_to_all | solution.py:70
  19.8 43.6 %all-gather.6.cloned.1.call-done = bf16[4096,256]{1,0:T(8,128)(2,1)} async-done(((bf16[128,256]{1,0:T(8,128)(2,1)}), bf16[4096,256]{1,0:T(8,128)(2,1)}) %all-gather.6.cloned.1.call-update) | async-done | bytes 2097168 | tf_op jit(solution)/shard_map/all_gather | solution.py:73
  64.6 49.3 %all-gather.4.cloned.1.call-done = bf16[4096,256]{1,0:T(8,128)(2,1)} async-done(((bf16[128,256]{1,0:T(8,128)(2,1)}), bf16[4096,256]{1,0:T(8,128)(2,1)}) %all-gather.4.cloned.1.call-update) | async-done | bytes 2097168 | tf_op jit(solution)/shard_map/all_gather | solution.py:72
  115.2 24.3 %while.27 = (s32[]{:T(128)}, bf16[4,512,128]{2,1,0:T(8,128)(2,1)S(1)}, s32[4,512]{1,0:T(4,128)S(1)}, s32[4096]{0:T(1024)S(1)}, s32[4,512]{1,0:T(4,128)S(1)}, /*i...) while((s32[]{:T(128)}, ...), condition=%wide.region_3.4_spmd.clone, body=%wide.region_0.3_spmd.clone.sunk | while | flops 1096875008 | bytes 27564136 | solution.py:36
  115.2 2.5 fusion.40
  121.3 2.5 fusion.40
  125.1 2.2 fusion.42
  127.4 2.5 fusion.40
  131.2 2.2 fusion.42
  133.4 2.5 fusion.40
  137.2 2.2 fusion.42
  140.3 77.1 %all-gather.8.cloned.1.call-done = bf16[32,2048,128]{2,1,0:T(8,128)(2,1)} async-done(((bf16[1,2048,128]{2,1,0:T(8,128)(2,1)}), bf16[32,2048,128]{2,1,0:T(8,128)(2,1)}) %all-gather.8.cloned.1.call-update) | async-done | bytes 16777232 | tf_op jit(solution)/shard_map/all_gather | solution.py:100
  217.4 2.4 broadcast_in_dim.18.clone
  219.9 174.8 %while.26 = (s32[]{:T(128)}, f32[32,2,64,256]{3,2,1,0:T(8,128)}, bf16[32,2048,128]{2,1,0:T(8,128)(2,1)}, bf16[2048,256]{1,0:T(8,128)(2,1)}, s32[]{:T(128)}, /*in...) while((s32[]{:T(128)}, f32[32,2,64,256]{3,2,1,0:T(8,128)}, ...), condition=%wide.region_5.6_spmd, body=%wide.region_4.5_spmd.sunk | while | flops 134742032 | bytes 10027344 | solution.py:116
  222.7 2.6 bitcast_dynamic-update-slice_fusion.2
  228.1 2.6 bitcast_dynamic-update-slice_fusion.2
  233.6 2.6 bitcast_dynamic-update-slice_fusion.2
  239.0 2.6 bitcast_dynamic-update-slice_fusion.2
  244.4 2.6 bitcast_dynamic-update-slice_fusion.2
  249.9 2.6 bitcast_dynamic-update-slice_fusion.2
  255.3 2.6 bitcast_dynamic-update-slice_fusion.2
  260.7 2.6 bitcast_dynamic-update-slice_fusion.2
  266.1 2.6 bitcast_dynamic-update-slice_fusion.2
  271.6 2.6 bitcast_dynamic-update-slice_fusion.2
  277.0 2.6 bitcast_dynamic-update-slice_fusion.2
  282.4 2.6 bitcast_dynamic-update-slice_fusion.2
  287.9 2.6 bitcast_dynamic-update-slice_fusion.2
  293.3 2.6 bitcast_dynamic-update-slice_fusion.2
  298.7 2.6 bitcast_dynamic-update-slice_fusion.2
  304.1 2.6 bitcast_dynamic-update-slice_fusion.2
  309.6 2.6 bitcast_dynamic-update-slice_fusion.2
  315.1 2.6 bitcast_dynamic-update-slice_fusion.2
  320.6 2.6 bitcast_dynamic-update-slice_fusion.2
  326.0 2.6 bitcast_dynamic-update-slice_fusion.2
  331.5 2.6 bitcast_dynamic-update-slice_fusion.2
  337.0 2.6 bitcast_dynamic-update-slice_fusion.2
  342.5 2.6 bitcast_dynamic-update-slice_fusion.2
  348.0 2.6 bitcast_dynamic-update-slice_fusion.2
  353.5 2.6 bitcast_dynamic-update-slice_fusion.2
  359.0 2.6 bitcast_dynamic-update-slice_fusion.2
  364.5 2.6 bitcast_dynamic-update-slice_fusion.2
  370.0 2.6 bitcast_dynamic-update-slice_fusion.2
  375.5 2.6 bitcast_dynamic-update-slice_fusion.2
  381.0 2.6 bitcast_dynamic-update-slice_fusion.2
  386.5 2.6 bitcast_dynamic-update-slice_fusion.2
  392.0 2.6 bitcast_dynamic-update-slice_fusion.2
  394.7 100.2 %all-reduce.1 = bf16[4096,256]{1,0:T(8,128)(2,1)S(1)} all-reduce(f32[4096,256]{1,0:T(8,128)} %bitcast.61), channel_id=1, replica_groups=mesh['tp'=2,'sp'=32,'dp'=4] {'tp'}, use_global_device_ids=true, to_apply=%region_6.7 | all-reduce | flops 1048576 | bytes 6291456 | tf_op jit(solution)/shard_map/psum | solution.py:119
  496.6 64.7 %psum.15 = f32[2048]{0:T(1024)S(1)} all-reduce(f32[2048]{0:T(1024)S(1)} %get-tuple-element.206), channel_id=1, replica_groups=mesh['tp'=2,'sp'=32,'dp'=4] {'sp'}, use_global_device_ids=true, to_apply=%region_8.9 | all-reduce | flops 2048 | bytes 16384 | tf_op jit(solution)/shard_map/psum | solution.py:124
  (104 shorter events, 108.5 us)
Async XLA Ops:
  7.2 12.3 %copy-start.2 = (s32[4096]{0:T(1024)S(1)}, s32[4096]{0:T(1024)}, u32[]{:S(2)}) copy-start(s32[4096]{0:T(1024)} %param.15) | copy-start | bytes 49156
  7.2 56.2 %all-gather.6.cloned.1.call-start = ((), (), s32[]{:S(2)}) async-start(), calls=%async_computation.2 | async-start | bytes 2162688 | tf_op jit(solution)/shard_map/all_gather | solution.py:73
  7.9 106.0 %all-gather.4.cloned.1.call-start = ((), (), s32[]{:S(2)}) async-start(), calls=%async_computation.1 | async-start | bytes 2162688 | tf_op jit(solution)/shard_map/all_gather | solution.py:72
  10.8 104.4 %all-to-all-start = ((bf16[32,64,128]{2,1,0:T(8,128)(2,1)}), bf16[32,64,128]{2,1,0:T(8,128)(2,1)S(1)}, u32[]{:S(2)}, u32[]{:S(2)}) async-start(bf16[32,64,128]{2,1,0:T(8,128)(2,1)} %bitcast.4), calls=%async_computation | async-start | bytes 1048576 | tf_op jit(solution)/shard_map/all_to_all | solution.py:70
  19.4 198.0 %all-gather.8.cloned.1.call-start = ((), (), s32[]{:S(2)}) async-start(), calls=%async_computation.3 | async-start | bytes 17301504 | tf_op jit(solution)/shard_map/all_gather | solution.py:100
  115.2 25.1 %copy-start.4 = (s32[256]{0:T(256)S(1)}, s32[256]{0:T(256)}, u32[]{:S(2)}) copy-start(s32[256]{0:T(256)} %param.19) | copy-start | bytes 3076
  139.5 0.8 copy-start.1
  394.7 166.6 %copy-start.3 = (f32[256]{0:T(256)S(1)}, f32[256]{0:T(256)}, u32[]{:S(2)}) copy-start(f32[256]{0:T(256)} %param.18) | copy-start | bytes 3076
  496.5 66.2 %copy-start = (bf16[2048,256]{1,0:T(8,128)(2,1)}, bf16[2048,256]{1,0:T(8,128)(2,1)S(1)}, u32[]{:S(2)}) copy-start(bf16[2048,256]{1,0:T(8,128)(2,1)S(1)} %get-tuple-element.207) | copy-start | bytes 3145732
Sparse Core Ops, SparseCore 0:
  10.5 52.7 all-gather.5
  65.9 47.9 all-gather.3
  140.4 76.9 all-gather.7
where the time goes:
time: 574 us; the launch traced here: 569 us
  waiting for transfers between devices  171 us (30%)
  blocking collectives  165 us (29%)
  matrix products  103 us (18%)
  local copies, waits for them, and re-layouts  98.9 us (17%)
  between operations  14 us (2%)
  starting transfers between devices  8.69 us (2%)
  other arithmetic  8.28 us (1%)
    psum x1, blocking collectives, body(): whole_sum = lax.psum(flattened, 'tp')  100 us
    dot_general x32, matrix products, add_one(): jnp.dot(chosen, head_weight, preferred_element_type=jnp.float32)  83.6 us
    all_gather x1, waiting for transfers between devices, body(): pieces = lax.all_gather(own_outputs, 'sp', axis=0, tiled=True)  77.1 us
    psum x1, blocking collectives, body(): square_sum = lax.psum(jnp.sum(widened * widened, axis=1), 'sp')  64.7 us
    dynamic_slice x32, local copies, waits for them, and re-layouts, add_one(): lax.dynamic_slice(current, corner, (sp_count, 1, half_rows, column_count))  56.2 us
    all_gather x1, waiting for transfers between devices, body(): lax.all_gather(key_projection_rows, 'sp', axis=0, tiled=True)  49.3 us
    all_gather x1, waiting for transfers between devices, body(): lax.all_gather(values, 'sp', axis=0, tiled=True)  43.6 us
    dynamic_slice x32, local copies, waits for them, and re-layouts, add_one(): chosen = lax.dynamic_index_in_dim(pieces, number, 0, keepdims=False)  34.6 us
  transfers between devices with their start and end apart: 4, of which 3 were waited for; matrix products, arithmetic and copies ran while one was open for 1% of the time, Pallas kernels for 0%

commit v1 on v0

--- a/solution.py
+++ b/solution.py
@@ -69,7 +69,10 @@
     ).reshape(item_count, half_rows, HEAD_DIMENSION)
     query_recv = lax.all_to_all(query_items, "sp", split_axis=0, concat_axis=1, tiled=True)
     key_all, value_all = (
-        lax.all_gather(key_projection_rows, "sp", axis=0, tiled=True),
+        jnp.concatenate(
+            lax.all_to_all(jnp.stack([key_projection_rows] * lax.axis_size("sp")), "sp", 0, 0),
+            axis=0,
+        ),
         lax.all_gather(values, "sp", axis=0, tiled=True),
     )
     key_pos = jnp.arange(window_token_rows, dtype=jnp.int32)

time: 574 us -> 542 us (0.944)
  waiting for transfers between devices: 171 us -> 127 us
  matrix products: 103 us -> 110 us
    all_gather x1 -> x0, waiting for transfers between devices: 49.3 us -> none  [body(): lax.all_gather(key_projection_rows, 'sp', axis=0, tiled=True)]
    all_to_all x0 -> x1, waiting for transfers between devices: none -> 27.8 us  [body(): lax.all_to_all(jnp.stack([key_projection_rows] * lax.axis_size('sp')), 's...]
    all_gather x1, waiting for transfers between devices: 43.6 us -> 20 us  [body(): lax.all_gather(values, 'sp', axis=0, tiled=True)]
    all_to_all x0 -> x1, starting transfers between devices: none -> 8.58 us  [body(): lax.all_to_all(jnp.stack([key_projection_rows] * lax.axis_size('sp')), 's...]
where the time goes in v1:
time: 542 us; the launch traced here: 537 us
  blocking collectives  165 us (30%)
  waiting for transfers between devices  127 us (23%)
  matrix products  110 us (20%)
  local copies, waits for them, and re-layouts  98.3 us (18%)
  between operations  14.3 us (3%)
  starting transfers between devices  13.7 us (3%)
  other arithmetic  8.25 us (2%)
    psum x1, blocking collectives, body(): whole_sum = lax.psum(flattened, 'tp')  100 us
    dot_general x32, matrix products, add_one(): jnp.dot(chosen, head_weight, preferred_element_type=jnp.float32)  84.7 us
    all_gather x1, waiting for transfers between devices, body(): pieces = lax.all_gather(own_outputs, 'sp', axis=0, tiled=True)  78.5 us
    psum x1, blocking collectives, body(): square_sum = lax.psum(jnp.sum(widened * widened, axis=1), 'sp')  64.7 us
    dynamic_slice x32, local copies, waits for them, and re-layouts, add_one(): lax.dynamic_slice(current, corner, (sp_count, 1, half_rows, column_count))  56.2 us
    dynamic_slice x32, local copies, waits for them, and re-layouts, add_one(): chosen = lax.dynamic_index_in_dim(pieces, number, 0, keepdims=False)  34.6 us
    all_to_all x1, waiting for transfers between devices, body(): lax.all_to_all(jnp.stack([key_projection_rows] * lax.axis_size('sp')), 's...  27.8 us
    all_gather x1, waiting for transfers between devices, body(): lax.all_gather(values, 'sp', axis=0, tiled=True)  20 us
  transfers between devices with their start and end apart: 4, of which 3 were waited for; matrix products, arithmetic and copies ran while one was open for 1% of the time, Pallas kernels for 0%

profile of v1, /device:TPU:1, one launch (start us, length us, event | category | flops | bytes accessed | tf_op | source)
XLA Modules:
  0.0 537.4 jit_solution(6444248883934384883)
XLA Ops:
  10.3 8.6 %all-to-all-start.1 = ((bf16[32,128,256]{2,1,0:T(8,128)(2,1)}), bf16[32,128,256]{2,1,0:T(8,128)(2,1)S(1)}, u32[]{:S(2)}, u32[]{:S(2)}) async-start(bf16[32,128,256]{2,1,0:T(8,128)(2,1)} %stack.2), calls=%async_computation.1 | async-start | bytes 4194304 | tf_op jit(solution)/shard_map/all_to_all | solution.py:73
  20.3 27.8 %all-to-all-done.1 = bf16[32,128,256]{2,1,0:T(8,128)(2,1)S(1)} async-done(((bf16[32,128,256]{2,1,0:T(8,128)(2,1)}), bf16[32,128,256]{2,1,0:T(8,128)(2,1)S(1)}, u32[]{:S(2)}, u32[]{:S(2)}) %all-to-all-start.1) | async-done | bytes 2097184 | tf_op jit(solution)/shard_map/all_to_all | solution.py:73
  48.2 5.0 all-to-all-start
  53.3 20.0 %all-gather.3.cloned.1.call-done = bf16[4096,256]{1,0:T(8,128)(2,1)} async-done(((bf16[128,256]{1,0:T(8,128)(2,1)}), bf16[4096,256]{1,0:T(8,128)(2,1)}) %all-gather.3.cloned.1.call-update) | async-done | bytes 2097168 | tf_op jit(solution)/shard_map/all_gather | solution.py:76
  74.7 31.0 %while.27 = (s32[]{:T(128)}, bf16[4,512,128]{2,1,0:T(8,128)(2,1)}, s32[4,512]{1,0:T(4,128)S(1)}, s32[4096]{0:T(1024)S(1)}, s32[4,512]{1,0:T(4,128)S(1)}, /*index...) while((s32[]{:T(128)}, bf16[4,512,128]{2,1,0:T(8,128)(2,1)}, ...), condition=%wide.region_3.4_spmd.clone, body=%wide.region_0.3_spmd.clone.sunk | while | flops 1096875008 | bytes 27565152 | solution.py:36
  74.7 3.6 fusion.40
  79.6 2.8 fusion.42
  82.4 3.6 fusion.40
  87.3 2.8 fusion.42
  90.2 3.6 fusion.40
  95.1 2.8 fusion.42
  97.9 3.6 fusion.40
  102.8 2.8 fusion.42
  105.7 78.5 %all-gather.5.cloned.1.call-done = bf16[32,2048,128]{2,1,0:T(8,128)(2,1)} async-done(((bf16[1,2048,128]{2,1,0:T(8,128)(2,1)}), bf16[32,2048,128]{2,1,0:T(8,128)(2,1)}) %all-gather.5.cloned.1.call-update) | async-done | bytes 16777232 | tf_op jit(solution)/shard_map/all_gather | solution.py:103
  186.6 175.9 %while.26 = (s32[]{:T(128)}, f32[32,2,64,256]{3,2,1,0:T(8,128)}, bf16[32,2048,128]{2,1,0:T(8,128)(2,1)}, bf16[2048,256]{1,0:T(8,128)(2,1)}, s32[]{:T(128)}, /*in...) while((s32[]{:T(128)}, f32[32,2,64,256]{3,2,1,0:T(8,128)}, ...), condition=%wide.region_5.6_spmd, body=%wide.region_4.5_spmd.sunk | while | flops 134742032 | bytes 10027344 | solution.py:119
  189.5 2.6 bitcast_dynamic-update-slice_fusion.2
  195.0 2.6 bitcast_dynamic-update-slice_fusion.2
  200.5 2.6 bitcast_dynamic-update-slice_fusion.2
  206.0 2.6 bitcast_dynamic-update-slice_fusion.2
  211.5 2.6 bitcast_dynamic-update-slice_fusion.2
  216.9 2.6 bitcast_dynamic-update-slice_fusion.2
  222.4 2.6 bitcast_dynamic-update-slice_fusion.2
  227.9 2.6 bitcast_dynamic-update-slice_fusion.2
  233.4 2.6 bitcast_dynamic-update-slice_fusion.2
  238.9 2.6 bitcast_dynamic-update-slice_fusion.2
  244.4 2.6 bitcast_dynamic-update-slice_fusion.2
  249.9 2.6 bitcast_dynamic-update-slice_fusion.2
  255.4 2.6 bitcast_dynamic-update-slice_fusion.2
  260.9 2.6 bitcast_dynamic-update-slice_fusion.2
  266.4 2.6 bitcast_dynamic-update-slice_fusion.2
  271.9 2.6 bitcast_dynamic-update-slice_fusion.2
  277.4 2.6 bitcast_dynamic-update-slice_fusion.2
  288.4 2.6 bitcast_dynamic-update-slice_fusion.2
  293.9 2.6 bitcast_dynamic-update-slice_fusion.2
  299.4 2.6 bitcast_dynamic-update-slice_fusion.2
  304.9 2.6 bitcast_dynamic-update-slice_fusion.2
  310.4 2.6 bitcast_dynamic-update-slice_fusion.2
  315.9 2.6 bitcast_dynamic-update-slice_fusion.2
  321.4 2.6 bitcast_dynamic-update-slice_fusion.2
  326.9 2.6 bitcast_dynamic-update-slice_fusion.2
  332.4 2.6 bitcast_dynamic-update-slice_fusion.2
  337.9 2.6 bitcast_dynamic-update-slice_fusion.2
  343.4 2.6 bitcast_dynamic-update-slice_fusion.2
  348.9 2.6 bitcast_dynamic-update-slice_fusion.2
  354.4 2.6 bitcast_dynamic-update-slice_fusion.2
  359.9 2.6 bitcast_dynamic-update-slice_fusion.2
  362.5 100.2 %all-reduce.1 = bf16[4096,256]{1,0:T(8,128)(2,1)S(1)} all-reduce(f32[4096,256]{1,0:T(8,128)} %bitcast.62), channel_id=1, replica_groups=mesh['tp'=2,'sp'=32,'dp'=4] {'tp'}, use_global_device_ids=true, to_apply=%region_6.7 | all-reduce | flops 1048576 | bytes 6291456 | tf_op jit(solution)/shard_map/psum | solution.py:122
  464.4 64.7 %psum.15 = f32[2048]{0:T(1024)S(1)} all-reduce(f32[2048]{0:T(1024)S(1)} %get-tuple-element.206), channel_id=1, replica_groups=mesh['tp'=2,'sp'=32,'dp'=4] {'sp'}, use_global_device_ids=true, to_apply=%region_8.9 | all-reduce | flops 2048 | bytes 16384 | tf_op jit(solution)/shard_map/psum | solution.py:127
  (104 shorter events, 109.9 us)
Async XLA Ops:
  7.2 11.8 %copy-start.2 = (s32[4096]{0:T(1024)S(1)}, s32[4096]{0:T(1024)}, u32[]{:S(2)}) copy-start(s32[4096]{0:T(1024)} %param.15) | copy-start | bytes 49156
  7.2 12.0 %copy-start.1 = (bf16[128,2048]{1,0:T(8,128)(2,1)S(1)}, bf16[128,2048]{1,0:T(8,128)(2,1)}, u32[]{:S(2)}) copy-start(bf16[128,2048]{1,0:T(8,128)(2,1)} %param.12) | copy-start | bytes 1572868
  7.2 66.2 %all-gather.3.cloned.1.call-start = ((), (), s32[]{:S(2)}) async-start(), calls=%async_computation.2 | async-start | bytes 2162688 | tf_op jit(solution)/shard_map/all_gather | solution.py:76
  10.3 37.9 %all-to-all-start.1 = ((bf16[32,128,256]{2,1,0:T(8,128)(2,1)}), bf16[32,128,256]{2,1,0:T(8,128)(2,1)S(1)}, u32[]{:S(2)}, u32[]{:S(2)}) async-start(bf16[32,128,256]{2,1,0:T(8,128)(2,1)} %stack.2), calls=%async_computation.1 | async-start | bytes 4194304 | tf_op jit(solution)/shard_map/all_to_all | solution.py:73
  48.2 26.5 %all-to-all-start = ((bf16[32,64,128]{2,1,0:T(8,128)(2,1)}), bf16[32,64,128]{2,1,0:T(8,128)(2,1)}, u32[]{:S(2)}, u32[]{:S(2)}) async-start(bf16[32,64,128]{2,1,0:T(8,128)(2,1)} %bitcast.4), calls=%async_computation | async-start | bytes 1048576 | tf_op jit(solution)/shard_map/all_to_all | solution.py:70
  53.2 131.0 %all-gather.5.cloned.1.call-start = ((), (), s32[]{:S(2)}) async-start(), calls=%async_computation.3 | async-start | bytes 17301504 | tf_op jit(solution)/shard_map/all_gather | solution.py:103
  74.7 31.0 %copy-start.4 = (s32[256]{0:T(256)S(1)}, s32[256]{0:T(256)}, u32[]{:S(2)}) copy-start(s32[256]{0:T(256)} %param.19) | copy-start | bytes 3076
  362.5 166.6 %copy-start.3 = (f32[256]{0:T(256)S(1)}, f32[256]{0:T(256)}, u32[]{:S(2)}) copy-start(f32[256]{0:T(256)} %param.18) | copy-start | bytes 3076
  464.4 66.2 %copy-start = (bf16[2048,256]{1,0:T(8,128)(2,1)}, bf16[2048,256]{1,0:T(8,128)(2,1)S(1)}, u32[]{:S(2)}) copy-start(bf16[2048,256]{1,0:T(8,128)(2,1)S(1)} %get-tuple-element.207) | copy-start | bytes 3145732
Sparse Core Ops, SparseCore 0:
  10.5 62.7 all-gather.2
  105.8 78.3 all-gather.4
